TPU v7x, 32 devices: a whole 2x2x4 slice. The times are simulated.
32 devices in a mesh: group: 4 (over x, core), member: 8 (over z, y).
Axes of the slice: x: 2, y: 2, z: 4, core: 2. Of those that a mesh axis runs over, the one named last changes fastest.
Arguments:
- activations: bfloat16 [8192, 1152], P(('group', 'member')), may hold values from -6 to 6
- routes: int32 [8192, 1], P(('group', 'member')), may hold values from 0 to 31; in each aligned block of 256 rows (0 to 255, 256 to 511, ...) at most 16 rows name the same one
- centre_bias: float32 [1152], replicated, may hold values from -2 to 2
- centre_first: float32 [1152], replicated, may hold values from -600 to 600
- centre_second: float32 [1152], replicated, may hold values from 1000 to 1000000
- router: bfloat16 [32, 1152], P(('group', 'member')), may hold values from -0.1875 to 0.1875
- router_first: float32 [32, 1152], P(('group', 'member')), may hold values from -180 to 180
- router_second: float32 [32, 1152], P(('group', 'member')), may hold values from 100 to 100000
- encoder: bfloat16 [32, 1152, 512], P(('group', 'member')), may hold values from -0.1875 to 0.1875
- enc_bias: float32 [32, 512], P(('group', 'member')), may hold values from -3 to 3
- decoder: bfloat16 [32, 512, 1152], P(('group', 'member')), may hold values from -0.25 to 0.25
- encoder_first: float32 [32, 1152, 512], P(('group', 'member')), may hold values from -30 to 30
- encoder_second: float32 [32, 1152, 512], P(('group', 'member')), may hold values from 1 to 1000
- enc_bias_first: float32 [32, 512], P(('group', 'member')), may hold values from -60 to 60
- enc_bias_second: float32 [32, 512], P(('group', 'member')), may hold values from 10 to 10000
- decoder_first: float32 [32, 512, 1152], P(('group', 'member')), may hold values from -30 to 30
- decoder_second: float32 [32, 512, 1152], P(('group', 'member')), may hold values from 1 to 1000
Outputs:
- recon: bfloat16 [8192, 1152], P(('group', 'member'))
- new_centre: float32 [1152], replicated
- new_centre_first: float32 [1152], replicated
- new_centre_second: float32 [1152], replicated
- new_router: bfloat16 [32, 1152], P(('group', 'member'))
- new_router_first: float32 [32, 1152], P(('group', 'member'))
- new_router_second: float32 [32, 1152], P(('group', 'member'))
- new_encoder: bfloat16 [32, 1152, 512], P(('group', 'member'))
- new_enc_bias: float32 [32, 512], P(('group', 'member'))
- new_decoder: bfloat16 [32, 512, 1152], P(('group', 'member'))
- new_encoder_first: float32 [32, 1152, 512], P(('group', 'member'))
- new_encoder_second: float32 [32, 1152, 512], P(('group', 'member'))
- new_enc_bias_first: float32 [32, 512], P(('group', 'member'))
- new_enc_bias_second: float32 [32, 512], P(('group', 'member'))
- new_decoder_first: float32 [32, 512, 1152], P(('group', 'member'))
- new_decoder_second: float32 [32, 512, 1152], P(('group', 'member'))
Inputs may be any that keep to these rules, and one draw needn't show every extreme that they name: `routes`: each row names the one expert that serves it. At most 16 rows of one device name the same expert, and in every draw some device's rows name some expert exactly 16 times.
All inputs are finite; a program needn't handle non-finite values.
Results may differ from a plain program's by a relative error of at most 0.009.
Values may be sent and summed in bfloat16 or wider, within the bound.
A program may use at most 128 MiB of HBM per device.

v0:
```python
import jax
import jax.numpy as jnp
from jax import lax
from jax.sharding import PartitionSpec as P

STEP = 10
learn_rate = 0.001
beta_one = 0.9
beta_two = 0.999
adam_eps = 1e-08
sparsity = 0.1


def adam_update(weights_in, gradient, moment_one, moment_two):
    first_new = beta_one * moment_one + (1.0 - beta_one) * gradient
    second_new = beta_two * moment_two + (1.0 - beta_two) * gradient * gradient
    first_hat = first_new / (1.0 - beta_one**STEP)
    second_hat = second_new / (1.0 - beta_two**STEP)
    stepped = weights_in.astype(jnp.float32) - learn_rate * first_hat / (
        jnp.sqrt(second_hat) + adam_eps
    )
    return (stepped.astype(weights_in.dtype), first_new, second_new)


def forward_pass(in_rows, centre_bias, router_row, encoder, enc_bias, decoder):
    centred = (in_rows.astype(jnp.float32) - centre_bias).astype(jnp.bfloat16)
    preact = jnp.dot(centred, encoder, preferred_element_type=jnp.float32) + enc_bias
    positive = jnp.maximum(preact, 0.0)
    latents = (positive * positive).astype(jnp.bfloat16)
    logits = jnp.dot(in_rows, router_row, preferred_element_type=jnp.float32)
    gating = jax.nn.sigmoid(logits)
    ungated = jnp.dot(latents, decoder, preferred_element_type=jnp.float32)
    rebuilt = centre_bias + gating[:, None] * ungated
    return (centred, positive, latents, gating, ungated, rebuilt)


def backward_pass(
    in_rows, live_mask, centred, positive, latents, gating, ungated, rebuilt, encoder, decoder
):
    errors = (in_rows.astype(jnp.float32) - rebuilt) * live_mask[:, None]
    backward = (-gating[:, None] * errors).astype(jnp.bfloat16)
    decoder_grad = jnp.dot(latents.T, backward, preferred_element_type=jnp.float32)
    latent_grad = jnp.dot(backward, decoder.T, preferred_element_type=jnp.float32) + sparsity
    preact_grad = (latent_grad * 2.0 * positive * live_mask[:, None]).astype(jnp.bfloat16)
    encoder_grad = jnp.dot(centred.T, preact_grad, preferred_element_type=jnp.float32)
    bias_grad = jnp.sum(preact_grad.astype(jnp.float32), axis=0)
    logit_grad = (-jnp.sum(errors * ungated, axis=1) * gating * (1.0 - gating)).astype(jnp.bfloat16)
    router_grad = jnp.dot(logit_grad, in_rows, preferred_element_type=jnp.float32)
    centre_part = -jnp.sum(errors, axis=0) - jnp.dot(
        encoder.astype(jnp.float32), bias_grad, precision=lax.Precision.HIGHEST
    )
    return (encoder_grad, bias_grad, decoder_grad, router_grad, centre_part)


def per_device(
    activations,
    routes,
    centre_bias,
    centre_first,
    centre_second,
    router,
    router_first,
    router_second,
    encoder,
    enc_bias,
    decoder,
    encoder_first,
    encoder_second,
    enc_bias_first,
    enc_bias_second,
    decoder_first,
    decoder_second,
):
    groups = lax.axis_size("group")
    members = lax.axis_size("member")
    devices = groups * members
    row_count = activations.shape[0]
    feature_count = activations.shape[1]
    slot_cap = 2 * row_count // devices
    route_ids = routes[:, 0]
    onehot = (route_ids[:, None] == jnp.arange(devices, dtype=jnp.int32)[None, :]).astype(
        jnp.float32
    )
    earlier = (jnp.arange(row_count)[:, None] > jnp.arange(row_count)[None, :]).astype(jnp.float32)
    before = jnp.dot(earlier, onehot, precision=lax.Precision.HIGHEST)
    slot_rank = jnp.sum(before * onehot, axis=1).astype(jnp.int32)
    position = route_ids * slot_cap + slot_rank
    packed = (
        jnp.zeros((devices * slot_cap, feature_count), jnp.bfloat16).at[position].set(activations)
    )
    filled = (
        jnp.zeros((devices * slot_cap,), jnp.bfloat16)
        .at[position]
        .set(jnp.ones((row_count,), jnp.bfloat16))
    )
    arrived, arrived_mask = (
        lax.all_to_all(
            packed.reshape(devices, slot_cap, feature_count),
            ("group", "member"),
            split_axis=0,
            concat_axis=0,
            tiled=True,
        ),
        lax.all_to_all(
            filled.reshape(devices, slot_cap),
            ("group", "member"),
            split_axis=0,
            concat_axis=0,
            tiled=True,
        ),
    )
    in_rows = arrived.reshape(devices * slot_cap, feature_count)
    live_mask = arrived_mask.reshape(devices * slot_cap).astype(jnp.float32)
    centred, positive, latents, gating, ungated, rebuilt = forward_pass(
        in_rows, centre_bias, router[0], encoder[0], enc_bias[0], decoder[0]
    )
    outgoing = rebuilt.astype(jnp.bfloat16)
    returned = lax.all_to_all(
        outgoing.reshape(devices, slot_cap, feature_count),
        ("group", "member"),
        split_axis=0,
        concat_axis=0,
        tiled=True,
    )
    recon = returned.reshape(devices * slot_cap, feature_count)[position]
    encoder_grad, bias_grad, decoder_grad, router_grad, centre_part = backward_pass(
        in_rows,
        live_mask,
        centred,
        positive,
        latents,
        gating,
        ungated,
        rebuilt,
        encoder[0],
        decoder[0],
    )
    router_new = adam_update(router[0], router_grad, router_first[0], router_second[0])
    encoder_new = adam_update(encoder[0], encoder_grad, encoder_first[0], encoder_second[0])
    bias_new = adam_update(enc_bias[0], bias_grad, enc_bias_first[0], enc_bias_second[0])
    decoder_new = adam_update(decoder[0], decoder_grad, decoder_first[0], decoder_second[0])
    centre_total = lax.psum(centre_part, ("group", "member"))
    centre_new = adam_update(centre_bias, centre_total, centre_first, centre_second)
    return (
        recon,
        centre_new[0],
        centre_new[1],
        centre_new[2],
        router_new[0][None],
        router_new[1][None],
        router_new[2][None],
        encoder_new[0][None],
        bias_new[0][None],
        decoder_new[0][None],
        encoder_new[1][None],
        encoder_new[2][None],
        bias_new[1][None],
        bias_new[2][None],
        decoder_new[1][None],
        decoder_new[2][None],
    )


def solution(mesh):
    placed = (
        P(("group", "member"), None),
        P(("group", "member"), None),
        P(),
        P(),
        P(),
        P(("group", "member"), None),
        P(("group", "member"), None),
        P(("group", "member"), None),
        P(("group", "member"), None, None),
        P(("group", "member"), None),
        P(("group", "member"), None, None),
        P(("group", "member"), None, None),
        P(("group", "member"), None, None),
        P(("group", "member"), None),
        P(("group", "member"), None),
        P(("group", "member"), None, None),
        P(("group", "member"), None, None),
    )
    return jax.shard_map(
        per_device,
        mesh=mesh,
        in_specs=placed,
        out_specs=(
            P(("group", "member"), None),
            P(),
            P(),
            P(),
            P(("group", "member"), None),
            P(("group", "member"), None),
            P(("group", "member"), None),
            P(("group", "member"), None, None),
            P(("group", "member"), None),
            P(("group", "member"), None, None),
            P(("group", "member"), None, None),
            P(("group", "member"), None, None),
            P(("group", "member"), None),
            P(("group", "member"), None),
            P(("group", "member"), None, None),
            P(("group", "member"), None, None),
        ),
        check_vma=False,
    )
```

profile of v0, /device:TPU:0, one launch (start us, length us, event | category | flops | bytes accessed | tf_op | source)
XLA Modules:
  0.0 127.9 jit_solution(12452941034543054141)
XLA Ops:
  0.7 1.0 fusion.22
  1.6 0.7 compare_select_fusion
  2.3 2.2 %scatter_custom_fusion.1 = bf16[512]{0:T(512)(128)(2,1)S(1)} fusion(s32[256]{0:T(256)S(1)} %bitcast.95, bf16[256]{0:T(256)(128)(2,1)S(1)} %broadcast.120, bf16[]{:T(256)} %constant.17.clone.1), kind=kCustom, calls=%fused_computation.76 | custom fusion | bytes 1026 | tf_op jit(solution)/shard_map/scatter | solution.py:94
  4.5 0.7 all_to_all.16
  5.2 7.3 %all-to-all-start.2 = ((bf16[32,1,16]{2,1,0:T(2,128)(2,1)}), bf16[32,1,16]{2,1,0:T(2,128)(2,1)S(1)}, u32[]{:S(2)}, u32[]{:S(2)}) async-start(bf16[32,1,16]{2,1,0:T(2,128)(2,1)} %all_to_all.16), calls=%async_computation.2 | async-start | bytes 32768 | tf_op jit(solution)/shard_map/all_to_all | solution.py:104
  12.5 3.4 %scatter_custom_fusion = bf16[512,1152]{1,0:T(8,128)(2,1)} fusion(s32[256]{0:T(256)S(1)} %bitcast.96, bf16[256,1152]{1,0:T(8,128)(2,1)} %param.17, bf16[]{:T(256)} %constant.17.clone.1), kind=kCustom, calls=%fused_computation.48 | custom fusion | bytes 1180160 | tf_op jit(solution)/shard_map/scatter | solution.py:89
  15.9 3.7 %all-to-all-done.2 = bf16[32,1,16]{2,1,0:T(2,128)(2,1)S(1)} async-done(((bf16[32,1,16]{2,1,0:T(2,128)(2,1)}), bf16[32,1,16]{2,1,0:T(2,128)(2,1)S(1)}, u32[]{:S(2)}, u32[]{:S(2)}) %all-to-all-start.2) | async-done | bytes 1056 | tf_op jit(solution)/shard_map/all_to_all | solution.py:104
  19.6 2.7 %all-to-all-start = ((bf16[32,16,1152]{2,1,0:T(8,128)(2,1)}), bf16[32,16,1152]{2,1,0:T(8,128)(2,1)S(1)}, u32[]{:S(2)}, u32[]{:S(2)}) async-start(bf16[32,16,1152]{2,1,0:T(8,128)(2,1)} %bitcast.3), calls=%async_computation | async-start | bytes 2359296 | tf_op jit(solution)/shard_map/all_to_all | solution.py:97
  22.3 0.6 reduce.2
  22.9 0.6 pad_clamp_fusion
  23.5 0.6 multiply_reduce_fusion.1
  24.2 0.1 reshape.108
  24.3 28.3 %all-to-all-done = bf16[32,16,1152]{2,1,0:T(8,128)(2,1)S(1)} async-done(((bf16[32,16,1152]{2,1,0:T(8,128)(2,1)}), bf16[32,16,1152]{2,1,0:T(8,128)(2,1)S(1)}, u32[]{:S(2)}, u32[]{:S(2)}) %all-to-all-start) | async-done | bytes 1179680 | tf_op jit(solution)/shard_map/all_to_all | solution.py:97
  52.6 0.4 fusion.36
  53.0 0.2 subtract_convert_fusion.2
  53.3 0.9 fusion.8
  54.1 0.4 copy-done.14
  54.5 3.2 %multiply_reduce_fusion = (f32[512]{0:T(512)S(1)}, f32[1152]{0:T(1024)}, bf16[512,1152]{1,0:T(8,128)(2,1)}, bf16[512,1152]{1,0:T(8,128)(2,1)}) fusion(f32[512]{0:T(512)S(1)} %reshape.108, f32[512]{0:T(512)S(1)} %get-tuple-element.28, f32[1152]{0:T(1024)S(1)} %copy-done.1, bf16[32,16,1152]{2,1,0:T(8,128)(2,1)S(1)} %all-to-all-done, ...), kind=kOutput, calls=%fused_computation.15 | convolution fusion | flops 610990464 | bytes 5784576 | tf_op jit(solution)/shard_map/dot_general | solution.py:32
  57.8 0.3 convolution_reduce_fusion
  58.1 2.7 %all-to-all-start.1 = ((bf16[32,16,1152]{2,1,0:T(8,128)(2,1)}), bf16[32,16,1152]{2,1,0:T(8,128)(2,1)S(1)}, u32[]{:S(2)}, u32[]{:S(2)}) async-start(bf16[32,16,1152]{2,1,0:T(8,128)(2,1)} %bitcast.90), calls=%async_computation.1 | async-start | bytes 2359296 | tf_op jit(solution)/shard_map/all_to_all | solution.py:118
  60.8 3.7 %convert_reduce_fusion = (f32[512]{0:T(512)S(1)}, bf16[512,512]{1,0:T(8,128)(2,1)}) fusion(f32[512]{0:T(512)} %copy-done.11, f32[512,512]{1,0:T(8,128)} %copy-done.15, bf16[512,1152]{1,0:T(8,128)(2,1)} %get-tuple-element.35, bf16[1,512,1152]{2,1,0:T(8,128)(2,1)} %param.27), kind=kOutput, calls=%fused_computation.42 | convolution fusion | flops 605814272 | bytes 3936256 | tf_op jit(solution)/shard_map/dot_general | solution.py:43
  64.5 1.0 fusion.23
  65.6 0.6 broadcast_in_dim.54
  66.2 0.6 broadcast_in_dim.55
  66.8 0.6 broadcast_in_dim.56
  67.4 0.6 negate_subtract_fusion
  68.0 41.9 %psum.7 = f32[1152]{0:T(1024)S(1)} all-reduce(f32[1152]{0:T(1024)} %negate_subtract_fusion), channel_id=1, replica_groups=mesh['group'=4,'member'=8] {'group','member'}, use_global_device_ids=true, to_apply=%region_5.0 | all-reduce | flops 1152 | bytes 9216 | tf_op jit(solution)/shard_map/psum | solution.py:142
  109.9 1.3 %divide_subtract_fusion.1 = (f32[1,512]{1,0:T(1,128)}, f32[1,512]{1,0:T(1,128)}, f32[1,512]{1,0:T(1,128)}) fusion(f32[1,512]{1,0:T(1,128)} %param.26, f32[1,512]{1,0:T(1,128)} %bitcast.93, f32[1,512]{1,0:T(1,128)} %param.30, f32[1,512]{1,0:T(1,128)} %param.31), kind=kLoop, calls=%fused_computation.72 | loop fusion | flops 6144 | bytes 14336 | tf_op jit(solution)/shard_map/sub | solution.py:19
  111.2 1.3 %divide_subtract_fusion = (f32[1152]{0:T(1024)}, f32[1152]{0:T(1024)}, f32[1152]{0:T(1024)}) fusion(f32[1152]{0:T(1024)S(1)} %copy-done.1, f32[1152]{0:T(1024)S(1)} %psum.7, f32[1152]{0:T(1024)} %param.20, f32[1152]{0:T(1024)} %param.21), kind=kLoop, calls=%fused_computation.61 | loop fusion | flops 13824 | bytes 32256 | tf_op jit(solution)/shard_map/sub | solution.py:19
  112.6 8.3 %fusion.28 = (f32[1,512,1152]{2,1,0:T(8,128)}, bf16[1,512,1152]{2,1,0:T(8,128)(2,1)}, f32[1,512,1152]{2,1,0:T(8,128)}) fusion(f32[1,512,1152]{2,1,0:T(8,128)} %param.33, f32[1,512,1152]{2,1,0:T(8,128)} %param.32, bf16[1,512,1152]{2,1,0:T(8,128)(2,1)} %param.27, bf16[512,1152]{1,0:T(8,128)(2,1)} %get-tuple-element.35, f32[512,512]{1,0:T(8,128)} %copy-done.15), kind=kOutput, calls=%fused_computation.46 | convolution fusion | flops 612761600 | bytes 14024704 | tf_op jit(solution)/shard_map/dot_general | solution.py:42
  120.9 4.8 %fusion.29 = (f32[1,1152,512]{2,1,0:T(8,128)}, bf16[1,1152,512]{2,1,0:T(8,128)(2,1)}, f32[1,1152,512]{2,1,0:T(8,128)}) fusion(f32[1,1152,512]{2,1,0:T(8,128)S(1)} %copy-done.12, f32[1,1152,512]{2,1,0:T(8,128)S(1)} %copy-done.13, bf16[1,1152,512]{2,1,0:T(8,128)(2,1)S(1)} %copy-done, bf16[512,512]{1,0:T(8,128)(2,1)S(1)} %copy-done.16, ...), kind=kOutput, calls=%fused_computation.47 | convolution fusion | flops 614006784 | bytes 13505024 | tf_op jit(solution)/shard_map/dot_general | solution.py:45
  125.7 2.2 %gather_fusion = bf16[256,1152]{1,0:T(8,128)(2,1)} fusion(bf16[512,1152]{1,0:T(8,128)(2,1)S(1)} %bitcast.86, s32[1024]{0:T(1024)} %pad_clamp_fusion), kind=kCustom, calls=%fused_computation | custom fusion | bytes 1180672 | tf_op jit(solution)/shard_map/gather | solution.py:125
  (41 shorter events, 0.2 us)
Async XLA Ops:
  0.6 21.6 %copy-start.4 = (bf16[1,1152]{1,0:T(2,128)(2,1)S(1)}, bf16[1,1152]{1,0:T(2,128)(2,1)}, u32[]{:S(2)}) copy-start(bf16[1,1152]{1,0:T(2,128)(2,1)} %param.22) | copy-start | bytes 6916
  0.7 22.9 %copy-start.8 = (f32[1,1152]{1,0:T(1,128)S(1)}, f32[1,1152]{1,0:T(1,128)}, u32[]{:S(2)}) copy-start(f32[1,1152]{1,0:T(1,128)} %param.24) | copy-start | bytes 13828
  0.7 22.9 %copy-start.9 = (f32[1,1152]{1,0:T(1,128)S(1)}, f32[1,1152]{1,0:T(1,128)}, u32[]{:S(2)}) copy-start(f32[1,1152]{1,0:T(1,128)} %param.23) | copy-start | bytes 13828
  5.2 14.4 %all-to-all-start.2 = ((bf16[32,1,16]{2,1,0:T(2,128)(2,1)}), bf16[32,1,16]{2,1,0:T(2,128)(2,1)S(1)}, u32[]{:S(2)}, u32[]{:S(2)}) async-start(bf16[32,1,16]{2,1,0:T(2,128)(2,1)} %all_to_all.16), calls=%async_computation.2 | async-start | bytes 32768 | tf_op jit(solution)/shard_map/all_to_all | solution.py:104
  12.5 40.5 %copy-start.1 = (f32[1152]{0:T(1024)S(1)}, f32[1152]{0:T(1024)}, u32[]{:S(2)}) copy-start(f32[1152]{0:T(1024)} %param.19) | copy-start | bytes 13828
  19.6 33.0 %all-to-all-start = ((bf16[32,16,1152]{2,1,0:T(8,128)(2,1)}), bf16[32,16,1152]{2,1,0:T(8,128)(2,1)S(1)}, u32[]{:S(2)}, u32[]{:S(2)}) async-start(bf16[32,16,1152]{2,1,0:T(8,128)(2,1)} %bitcast.3), calls=%async_computation | async-start | bytes 2359296 | tf_op jit(solution)/shard_map/all_to_all | solution.py:97
  22.3 30.9 %copy-start = (bf16[1,1152,512]{2,1,0:T(8,128)(2,1)S(1)}, bf16[1,1152,512]{2,1,0:T(8,128)(2,1)}, u32[]{:S(2)}) copy-start(bf16[1,1152,512]{2,1,0:T(8,128)(2,1)} %param.25) | copy-start | bytes 3538948
  22.3 30.9 %copy-start.10 = (f32[1,512]{1,0:T(1,128)S(1)}, f32[1,512]{1,0:T(1,128)}, u32[]{:S(2)}) copy-start(f32[1,512]{1,0:T(1,128)} %param.26) | copy-start | bytes 6148
  24.3 29.8 %copy-start.11 = (f32[512]{0:T(512)}, f32[512]{0:T(512)S(1)}, u32[]{:S(2)}) copy-start(f32[512]{0:T(512)S(1)} %reshape.108) | copy-start | bytes 6148
  53.2 1.3 copy-start.14
  54.1 3.7 %copy-start.15 = (f32[512,512]{1,0:T(8,128)}, f32[512,512]{1,0:T(8,128)S(1)}, u32[]{:S(2)}) copy-start(f32[512,512]{1,0:T(8,128)S(1)} %fusion.8) | copy-start | bytes 3145732
  58.1 67.7 %all-to-all-start.1 = ((bf16[32,16,1152]{2,1,0:T(8,128)(2,1)}), bf16[32,16,1152]{2,1,0:T(8,128)(2,1)S(1)}, u32[]{:S(2)}, u32[]{:S(2)}) async-start(bf16[32,16,1152]{2,1,0:T(8,128)(2,1)} %bitcast.90), calls=%async_computation.1 | async-start | bytes 2359296 | tf_op jit(solution)/shard_map/all_to_all | solution.py:118
  60.7 3.7 %copy-start.2 = (f32[1152]{0:T(1024)S(1)}, f32[1152]{0:T(1024)}, u32[]{:S(2)}) copy-start(f32[1152]{0:T(1024)} %get-tuple-element.39) | copy-start | bytes 13828
  60.7 3.7 %copy-start.3 = (f32[1152]{0:T(1024)S(1)}, f32[1152]{0:T(1024)}, u32[]{:S(2)}) copy-start(f32[1152]{0:T(1024)} %get-tuple-element.40) | copy-start | bytes 13828
  60.8 3.7 %copy-start.5 = (bf16[1152]{0:T(1024)(128)(2,1)S(1)}, bf16[1152]{0:T(1024)(128)(2,1)}, u32[]{:S(2)}) copy-start(bf16[1152]{0:T(1024)(128)(2,1)} %reduce.2) | copy-start | bytes 6916
  60.8 6.6 %copy-start.7 = (f32[1152]{0:T(1024)S(1)}, f32[1152]{0:T(1024)}, u32[]{:S(2)}) copy-start(f32[1152]{0:T(1024)} %get-tuple-element.17) | copy-start | bytes 13828
  64.5 2.9 %copy-start.6 = (f32[512]{0:T(512)}, f32[512]{0:T(512)S(1)}, u32[]{:S(2)}) copy-start(f32[512]{0:T(512)S(1)} %get-tuple-element.37) | copy-start | bytes 6148
  112.5 8.3 %copy-start.12 = (f32[1,1152,512]{2,1,0:T(8,128)S(1)}, f32[1,1152,512]{2,1,0:T(8,128)}, u32[]{:S(2)}) copy-start(f32[1,1152,512]{2,1,0:T(8,128)} %param.29) | copy-start | bytes 7077892
  112.5 8.3 %copy-start.13 = (f32[1,1152,512]{2,1,0:T(8,128)S(1)}, f32[1,1152,512]{2,1,0:T(8,128)}, u32[]{:S(2)}) copy-start(f32[1,1152,512]{2,1,0:T(8,128)} %param.28) | copy-start | bytes 7077892
  112.6 8.3 %copy-start.16 = (bf16[512,512]{1,0:T(8,128)(2,1)S(1)}, bf16[512,512]{1,0:T(8,128)(2,1)}, u32[]{:S(2)}) copy-start(bf16[512,512]{1,0:T(8,128)(2,1)} %get-tuple-element.38) | copy-start | bytes 1572868
where the time goes:
time: 129 us; the launch traced here: 128 us
  blocking collectives  41.9 us (32%)
  waiting for transfers between devices  32 us (25%)
  matrix products  23.6 us (18%)
  starting transfers between devices  12.7 us (10%)
  local copies, waits for them, and re-layouts  10.8 us (8%)
  other arithmetic  6.11 us (5%)
    psum x1, blocking collectives, per_device(): centre_total = lax.psum(centre_part, ('group', 'member'))  41.9 us
    all_to_all x1, waiting for transfers between devices, per_device(): lax.all_to_all(packed.reshape(devices, slot_cap, feature_count), ('group'...  28.3 us
    dot_general x1, matrix products, backward_pass(): jnp.dot(latents.T, backward, preferred_element_type=jnp.float32)  8.33 us
    all_to_all x1, starting transfers between devices, per_device(): lax.all_to_all(filled.reshape(devices, slot_cap), ('group', 'member'), sp...  7.33 us
    dot_general x1, matrix products, backward_pass(): jnp.dot(centred.T, preact_grad, preferred_element_type=jnp.float32)  4.83 us
    all_to_all x1, waiting for transfers between devices, per_device(): lax.all_to_all(filled.reshape(devices, slot_cap), ('group', 'member'), sp...  3.7 us
    dot_general x1, matrix products, backward_pass(): jnp.dot(backward, decoder.T, preferred_element_type=jnp.float32) + sparsity  3.69 us
    scatter x1, local copies, waits for them, and re-layouts, per_device(): jnp.zeros((devices * slot_cap, feature_count), jnp.bfloat16).at[position]  3.35 us
  transfers between devices with their start and end apart: 3, of which 2 were waited for; matrix products, arithmetic and copies ran while one was open for 22% of the time, Pallas kernels for 0%

commit v1 on v0

--- a/solution.py
+++ b/solution.py
@@ -139,7 +139,7 @@
     encoder_new = adam_update(encoder[0], encoder_grad, encoder_first[0], encoder_second[0])
     bias_new = adam_update(enc_bias[0], bias_grad, enc_bias_first[0], enc_bias_second[0])
     decoder_new = adam_update(decoder[0], decoder_grad, decoder_first[0], decoder_second[0])
-    centre_total = lax.psum(centre_part, ("group", "member"))
+    centre_total = lax.psum(lax.psum(centre_part, "member"), "group")
     centre_new = adam_update(centre_bias, centre_total, centre_first, centre_second)
     return (
         recon,

time: 129 us -> 122 us (0.946)
  blocking collectives: 41.9 us -> 34.7 us
    psum x1 -> x2, blocking collectives: 41.9 us -> 34.7 us  [per_device(): centre_total = lax.psum(lax.psum(centre_part, 'member'), 'group')]
  transfers between devices with their start and end apart: 3 -> 3, of which waited for: 2 -> 2; matrix products, arithmetic and copies ran while one was open for 22% -> 23% of each run, Pallas kernels for 0% -> 0%
where the time goes in v1:
time: 122 us; the launch traced here: 120 us
  blocking collectives  34.7 us (28%)
  waiting for transfers between devices  32 us (26%)
  matrix products  23.6 us (19%)
  starting transfers between devices  12.7 us (10%)
  local copies, waits for them, and re-layouts  10.8 us (9%)
  other arithmetic  5.51 us (5%)
    psum x2, blocking collectives, per_device(): centre_total = lax.psum(lax.psum(centre_part, 'member'), 'group')  34.7 us
    all_to_all x1, waiting for transfers between devices, per_device(): lax.all_to_all(packed.reshape(devices, slot_cap, feature_count), ('group'...  28.3 us
    dot_general x1, matrix products, backward_pass(): jnp.dot(latents.T, backward, preferred_element_type=jnp.float32)  8.32 us
    all_to_all x1, starting transfers between devices, per_device(): lax.all_to_all(filled.reshape(devices, slot_cap), ('group', 'member'), sp...  7.33 us
    dot_general x1, matrix products, backward_pass(): jnp.dot(centred.T, preact_grad, preferred_element_type=jnp.float32)  4.83 us
    all_to_all x1, waiting for transfers between devices, per_device(): lax.all_to_all(filled.reshape(devices, slot_cap), ('group', 'member'), sp...  3.7 us
    dot_general x1, matrix products, backward_pass(): jnp.dot(backward, decoder.T, preferred_element_type=jnp.float32) + sparsity  3.69 us
    scatter x1, local copies, waits for them, and re-layouts, per_device(): jnp.zeros((devices * slot_cap, feature_count), jnp.bfloat16).at[position]  3.35 us
  transfers between devices with their start and end apart: 3, of which 2 were waited for; matrix products, arithmetic and copies ran while one was open for 23% of the time, Pallas kernels for 0%

profile of v1, /device:TPU:0, one launch (start us, length us, event | category | flops | bytes accessed | tf_op | source)
XLA Modules:
  0.0 120.1 jit_solution(12944510627616030664)
XLA Ops:
  0.7 1.0 fusion.22
  1.6 0.7 compare_select_fusion
  2.3 2.2 %scatter_custom_fusion.1 = bf16[512]{0:T(512)(128)(2,1)S(1)} fusion(s32[256]{0:T(256)S(1)} %bitcast.95, bf16[256]{0:T(256)(128)(2,1)S(1)} %broadcast.120, bf16[]{:T(256)} %constant.17.clone.1), kind=kCustom, calls=%fused_computation.76 | custom fusion | bytes 1026 | tf_op jit(solution)/shard_map/scatter | solution.py:94
  4.5 0.7 all_to_all.16
  5.2 7.3 %all-to-all-start.2 = ((bf16[32,1,16]{2,1,0:T(2,128)(2,1)}), bf16[32,1,16]{2,1,0:T(2,128)(2,1)S(1)}, u32[]{:S(2)}, u32[]{:S(2)}) async-start(bf16[32,1,16]{2,1,0:T(2,128)(2,1)} %all_to_all.16), calls=%async_computation.2 | async-start | bytes 32768 | tf_op jit(solution)/shard_map/all_to_all | solution.py:104
  12.5 3.4 %scatter_custom_fusion = bf16[512,1152]{1,0:T(8,128)(2,1)} fusion(s32[256]{0:T(256)S(1)} %bitcast.96, bf16[256,1152]{1,0:T(8,128)(2,1)} %param.17, bf16[]{:T(256)} %constant.17.clone.1), kind=kCustom, calls=%fused_computation.48 | custom fusion | bytes 1180160 | tf_op jit(solution)/shard_map/scatter | solution.py:89
  15.9 3.7 %all-to-all-done.2 = bf16[32,1,16]{2,1,0:T(2,128)(2,1)S(1)} async-done(((bf16[32,1,16]{2,1,0:T(2,128)(2,1)}), bf16[32,1,16]{2,1,0:T(2,128)(2,1)S(1)}, u32[]{:S(2)}, u32[]{:S(2)}) %all-to-all-start.2) | async-done | bytes 1056 | tf_op jit(solution)/shard_map/all_to_all | solution.py:104
  19.6 2.7 %all-to-all-start = ((bf16[32,16,1152]{2,1,0:T(8,128)(2,1)}), bf16[32,16,1152]{2,1,0:T(8,128)(2,1)S(1)}, u32[]{:S(2)}, u32[]{:S(2)}) async-start(bf16[32,16,1152]{2,1,0:T(8,128)(2,1)} %bitcast.3), calls=%async_computation | async-start | bytes 2359296 | tf_op jit(solution)/shard_map/all_to_all | solution.py:97
  22.3 0.6 reduce.2
  22.9 0.6 pad_clamp_fusion
  23.5 0.6 multiply_reduce_fusion.1
  24.2 0.1 reshape.108
  24.3 28.3 %all-to-all-done = bf16[32,16,1152]{2,1,0:T(8,128)(2,1)S(1)} async-done(((bf16[32,16,1152]{2,1,0:T(8,128)(2,1)}), bf16[32,16,1152]{2,1,0:T(8,128)(2,1)S(1)}, u32[]{:S(2)}, u32[]{:S(2)}) %all-to-all-start) | async-done | bytes 1179680 | tf_op jit(solution)/shard_map/all_to_all | solution.py:97
  52.6 0.4 fusion.36
  53.0 0.2 subtract_convert_fusion.2
  53.3 0.9 fusion.8
  54.1 0.4 copy-done.14
  54.5 3.2 %multiply_reduce_fusion = (f32[512]{0:T(512)S(1)}, f32[1152]{0:T(1024)}, bf16[512,1152]{1,0:T(8,128)(2,1)}, bf16[512,1152]{1,0:T(8,128)(2,1)}) fusion(f32[512]{0:T(512)S(1)} %reshape.108, f32[512]{0:T(512)S(1)} %get-tuple-element.28, f32[1152]{0:T(1024)S(1)} %copy-done.1, bf16[32,16,1152]{2,1,0:T(8,128)(2,1)S(1)} %all-to-all-done, ...), kind=kOutput, calls=%fused_computation.15 | convolution fusion | flops 610990464 | bytes 5784576 | tf_op jit(solution)/shard_map/dot_general | solution.py:32
  57.8 0.3 convolution_reduce_fusion
  58.0 2.7 %all-to-all-start.1 = ((bf16[32,16,1152]{2,1,0:T(8,128)(2,1)}), bf16[32,16,1152]{2,1,0:T(8,128)(2,1)S(1)}, u32[]{:S(2)}, u32[]{:S(2)}) async-start(bf16[32,16,1152]{2,1,0:T(8,128)(2,1)} %bitcast.90), calls=%async_computation.1 | async-start | bytes 2359296 | tf_op jit(solution)/shard_map/all_to_all | solution.py:118
  60.8 3.7 %convert_reduce_fusion = (f32[512]{0:T(512)S(1)}, bf16[512,512]{1,0:T(8,128)(2,1)}) fusion(f32[512]{0:T(512)} %copy-done.11, f32[512,512]{1,0:T(8,128)} %copy-done.15, bf16[512,1152]{1,0:T(8,128)(2,1)} %get-tuple-element.35, bf16[1,512,1152]{2,1,0:T(8,128)(2,1)} %param.27), kind=kOutput, calls=%fused_computation.42 | convolution fusion | flops 605814272 | bytes 3936256 | tf_op jit(solution)/shard_map/dot_general | solution.py:43
  64.5 1.0 fusion.23
  65.6 0.6 broadcast_in_dim.54
  66.1 0.6 broadcast_in_dim.55
  66.7 0.6 broadcast_in_dim.56
  67.4 28.7 %psum.14 = f32[1152]{0:T(1024)} all-reduce(f32[1152]{0:T(1024)S(1)} %negate_subtract_fusion), channel_id=1, replica_groups=mesh['group'=4,'member'=8] {'member'}, use_global_device_ids=true, to_apply=%region_5.0 | all-reduce | flops 1152 | bytes 9216 | tf_op jit(solution)/shard_map/psum | solution.py:142
  96.0 6.0 %psum.15 = f32[1152]{0:T(1024)S(1)} all-reduce(f32[1152]{0:T(1024)} %psum.14), channel_id=1, replica_groups=mesh['group'=4,'member'=8] {'group'}, use_global_device_ids=true, to_apply=%region_6.0 | all-reduce | flops 1152 | bytes 9216 | tf_op jit(solution)/shard_map/psum | solution.py:142
  102.1 1.3 %divide_subtract_fusion.1 = (f32[1,512]{1,0:T(1,128)}, f32[1,512]{1,0:T(1,128)}, f32[1,512]{1,0:T(1,128)}) fusion(f32[1,512]{1,0:T(1,128)} %param.26, f32[1,512]{1,0:T(1,128)} %bitcast.93, f32[1,512]{1,0:T(1,128)} %param.30, f32[1,512]{1,0:T(1,128)} %param.31), kind=kLoop, calls=%fused_computation.72 | loop fusion | flops 6144 | bytes 14336 | tf_op jit(solution)/shard_map/sub | solution.py:19
  103.4 1.3 %divide_subtract_fusion = (f32[1152]{0:T(1024)}, f32[1152]{0:T(1024)}, f32[1152]{0:T(1024)}) fusion(f32[1152]{0:T(1024)S(1)} %copy-done.1, f32[1152]{0:T(1024)S(1)} %psum.15, f32[1152]{0:T(1024)} %param.20, f32[1152]{0:T(1024)} %param.21), kind=kLoop, calls=%fused_computation.61 | loop fusion | flops 13824 | bytes 32256 | tf_op jit(solution)/shard_map/sub | solution.py:19
  104.8 8.3 %fusion.28 = (f32[1,512,1152]{2,1,0:T(8,128)}, bf16[1,512,1152]{2,1,0:T(8,128)(2,1)}, f32[1,512,1152]{2,1,0:T(8,128)}) fusion(f32[1,512,1152]{2,1,0:T(8,128)} %param.33, f32[1,512,1152]{2,1,0:T(8,128)} %param.32, bf16[1,512,1152]{2,1,0:T(8,128)(2,1)} %param.27, bf16[512,1152]{1,0:T(8,128)(2,1)} %get-tuple-element.35, f32[512,512]{1,0:T(8,128)} %copy-done.15), kind=kOutput, calls=%fused_computation.46 | convolution fusion | flops 612761600 | bytes 14024704 | tf_op jit(solution)/shard_map/dot_general | solution.py:42
  113.1 4.8 %fusion.29 = (f32[1,1152,512]{2,1,0:T(8,128)}, bf16[1,1152,512]{2,1,0:T(8,128)(2,1)}, f32[1,1152,512]{2,1,0:T(8,128)}) fusion(f32[1,1152,512]{2,1,0:T(8,128)S(1)} %copy-done.12, f32[1,1152,512]{2,1,0:T(8,128)S(1)} %copy-done.13, bf16[1,1152,512]{2,1,0:T(8,128)(2,1)S(1)} %copy-done, bf16[512,512]{1,0:T(8,128)(2,1)S(1)} %copy-done.16, ...), kind=kOutput, calls=%fused_computation.47 | convolution fusion | flops 614006784 | bytes 13505024 | tf_op jit(solution)/shard_map/dot_general | solution.py:45
  117.9 2.2 %gather_fusion = bf16[256,1152]{1,0:T(8,128)(2,1)} fusion(bf16[512,1152]{1,0:T(8,128)(2,1)S(1)} %bitcast.86, s32[1024]{0:T(1024)} %pad_clamp_fusion), kind=kCustom, calls=%fused_computation | custom fusion | bytes 1180672 | tf_op jit(solution)/shard_map/gather | solution.py:125
  (42 shorter events, 0.2 us)
Async XLA Ops:
  0.6 21.6 %copy-start.4 = (bf16[1,1152]{1,0:T(2,128)(2,1)S(1)}, bf16[1,1152]{1,0:T(2,128)(2,1)}, u32[]{:S(2)}) copy-start(bf16[1,1152]{1,0:T(2,128)(2,1)} %param.22) | copy-start | bytes 6916
  0.7 22.9 %copy-start.8 = (f32[1,1152]{1,0:T(1,128)S(1)}, f32[1,1152]{1,0:T(1,128)}, u32[]{:S(2)}) copy-start(f32[1,1152]{1,0:T(1,128)} %param.24) | copy-start | bytes 13828
  0.7 22.9 %copy-start.9 = (f32[1,1152]{1,0:T(1,128)S(1)}, f32[1,1152]{1,0:T(1,128)}, u32[]{:S(2)}) copy-start(f32[1,1152]{1,0:T(1,128)} %param.23) | copy-start | bytes 13828
  5.2 14.4 %all-to-all-start.2 = ((bf16[32,1,16]{2,1,0:T(2,128)(2,1)}), bf16[32,1,16]{2,1,0:T(2,128)(2,1)S(1)}, u32[]{:S(2)}, u32[]{:S(2)}) async-start(bf16[32,1,16]{2,1,0:T(2,128)(2,1)} %all_to_all.16), calls=%async_computation.2 | async-start | bytes 32768 | tf_op jit(solution)/shard_map/all_to_all | solution.py:104
  12.5 40.5 %copy-start.1 = (f32[1152]{0:T(1024)S(1)}, f32[1152]{0:T(1024)}, u32[]{:S(2)}) copy-start(f32[1152]{0:T(1024)} %param.19) | copy-start | bytes 13828
  19.6 33.0 %all-to-all-start = ((bf16[32,16,1152]{2,1,0:T(8,128)(2,1)}), bf16[32,16,1152]{2,1,0:T(8,128)(2,1)S(1)}, u32[]{:S(2)}, u32[]{:S(2)}) async-start(bf16[32,16,1152]{2,1,0:T(8,128)(2,1)} %bitcast.3), calls=%async_computation | async-start | bytes 2359296 | tf_op jit(solution)/shard_map/all_to_all | solution.py:97
  22.3 30.9 %copy-start = (bf16[1,1152,512]{2,1,0:T(8,128)(2,1)S(1)}, bf16[1,1152,512]{2,1,0:T(8,128)(2,1)}, u32[]{:S(2)}) copy-start(bf16[1,1152,512]{2,1,0:T(8,128)(2,1)} %param.25) | copy-start | bytes 3538948
  22.3 30.9 %copy-start.10 = (f32[1,512]{1,0:T(1,128)S(1)}, f32[1,512]{1,0:T(1,128)}, u32[]{:S(2)}) copy-start(f32[1,512]{1,0:T(1,128)} %param.26) | copy-start | bytes 6148
  24.3 29.8 %copy-start.11 = (f32[512]{0:T(512)}, f32[512]{0:T(512)S(1)}, u32[]{:S(2)}) copy-start(f32[512]{0:T(512)S(1)} %reshape.108) | copy-start | bytes 6148
  53.2 1.3 %copy-start.14 = (bf16[1,512,1152]{2,1,0:T(8,128)(2,1)S(1)}, bf16[1,512,1152]{2,1,0:T(8,128)(2,1)}, u32[]{:S(2)}) copy-start(bf16[1,512,1152]{2,1,0:T(8,128)(2,1)} %param.27) | copy-start | bytes 3538948
  54.1 3.6 %copy-start.15 = (f32[512,512]{1,0:T(8,128)}, f32[512,512]{1,0:T(8,128)S(1)}, u32[]{:S(2)}) copy-start(f32[512,512]{1,0:T(8,128)S(1)} %fusion.8) | copy-start | bytes 3145732
  58.0 59.9 %all-to-all-start.1 = ((bf16[32,16,1152]{2,1,0:T(8,128)(2,1)}), bf16[32,16,1152]{2,1,0:T(8,128)(2,1)S(1)}, u32[]{:S(2)}, u32[]{:S(2)}) async-start(bf16[32,16,1152]{2,1,0:T(8,128)(2,1)} %bitcast.90), calls=%async_computation.1 | async-start | bytes 2359296 | tf_op jit(solution)/shard_map/all_to_all | solution.py:118
  60.7 3.7 %copy-start.2 = (f32[1152]{0:T(1024)S(1)}, f32[1152]{0:T(1024)}, u32[]{:S(2)}) copy-start(f32[1152]{0:T(1024)} %get-tuple-element.39) | copy-start | bytes 13828
  60.7 3.7 %copy-start.3 = (f32[1152]{0:T(1024)S(1)}, f32[1152]{0:T(1024)}, u32[]{:S(2)}) copy-start(f32[1152]{0:T(1024)} %get-tuple-element.40) | copy-start | bytes 13828
  60.8 3.7 %copy-start.5 = (bf16[1152]{0:T(1024)(128)(2,1)S(1)}, bf16[1152]{0:T(1024)(128)(2,1)}, u32[]{:S(2)}) copy-start(bf16[1152]{0:T(1024)(128)(2,1)} %reduce.2) | copy-start | bytes 6916
  60.8 6.6 %copy-start.7 = (f32[1152]{0:T(1024)S(1)}, f32[1152]{0:T(1024)}, u32[]{:S(2)}) copy-start(f32[1152]{0:T(1024)} %get-tuple-element.17) | copy-start | bytes 13828
  64.5 2.9 %copy-start.6 = (f32[512]{0:T(512)}, f32[512]{0:T(512)S(1)}, u32[]{:S(2)}) copy-start(f32[512]{0:T(512)S(1)} %get-tuple-element.37) | copy-start | bytes 6148
  104.8 8.3 %copy-start.12 = (f32[1,1152,512]{2,1,0:T(8,128)S(1)}, f32[1,1152,512]{2,1,0:T(8,128)}, u32[]{:S(2)}) copy-start(f32[1,1152,512]{2,1,0:T(8,128)} %param.29) | copy-start | bytes 7077892
  104.8 8.3 %copy-start.13 = (f32[1,1152,512]{2,1,0:T(8,128)S(1)}, f32[1,1152,512]{2,1,0:T(8,128)}, u32[]{:S(2)}) copy-start(f32[1,1152,512]{2,1,0:T(8,128)} %param.28) | copy-start | bytes 7077892
  104.8 8.3 %copy-start.16 = (bf16[512,512]{1,0:T(8,128)(2,1)S(1)}, bf16[512,512]{1,0:T(8,128)(2,1)}, u32[]{:S(2)}) copy-start(bf16[512,512]{1,0:T(8,128)(2,1)} %get-tuple-element.38) | copy-start | bytes 1572868
